TPU v7x, 32 devices: a whole 2x2x4 slice. The times are simulated.
32 devices in a mesh: dp: 8 (over z, core), ctx: 4 (over y, x).
Axes of the slice: x: 2, y: 2, z: 4, core: 2. Of those that a mesh axis runs over, the one named last changes fastest.
Arguments:
- video: bfloat16 [64, 32, 64, 128], P('dp', 'ctx'), parts along dimension 0, may hold values from -6 to 6
- conv_weight: bfloat16 [3, 3, 3, 128, 256], replicated, may hold values from -0.109375 to 0.109375
- latent_weight: bfloat16 [256, 16], replicated, may hold values from -0.375 to 0.375
- embed_weight: bfloat16 [64, 3072], replicated, may hold values from -0.75 to 0.75
- modulation: float32 [32, 3072], P('dp'), parts along dimension 0, may hold values from -3 to 3
- qkv_weight: bfloat16 [3072, 3, 2048], P(None, None, 'ctx'), may hold values from -0.109375 to 0.109375
- qk_gain: float32 [2, 128], replicated, may hold values from 0.5 to 2
- text: bfloat16 [2048, 3072], P('dp'), parts along dimension 0, may hold values from -6 to 6
- text_weight: bfloat16 [3072, 2, 2048], P(None, None, 'ctx'), may hold values from -0.109375 to 0.109375
Outputs:
- attended: bfloat16 [8192, 2048], P(('dp', 'ctx')), parts along dimension 0
There are 8 independent parts, one for each index of `dp`. A program takes and returns all parts, laid end to end along the dimension named above; an argument that names none is the same for every part. Nothing has to cross between parts.
All inputs are finite; a program needn't handle non-finite values.
Results may differ from a plain program's by a relative error of at most 0.0074.
Values may be sent and summed in bfloat16 or wider, within the bound.
No kernel may reach another device: no remote copies, remote signals or barrier semaphores. Data moves between devices by JAX's collectives and lax.ppermute only.
A program may use at most 128 MiB of HBM per device.

v0:
```python
import math
import jax
import jax.numpy as jnp
from jax import lax
from jax.sharding import PartitionSpec as P

D = 3072
HS = 128


def shifted(x, axis, by):
    devices = lax.axis_size(axis)
    pairs = [(i, i + by) for i in range(devices) if 0 <= i + by < devices]
    return lax.ppermute(x, axis, pairs)


def layer_norm(values):
    centred = values - jnp.mean(values, -1, keepdims=True)
    return centred * lax.rsqrt(jnp.mean(centred * centred, -1, keepdims=True) + 1e-06)


def head_norm(values, gain):
    return values * lax.rsqrt(jnp.mean(values * values, -1, keepdims=True) + 1e-06) * gain


def patchify(latent):
    frames, rows, cols, chans = latent.shape
    shaped = latent.reshape(frames, rows // 2, 2, cols // 2, 2, chans)
    return shaped.transpose(0, 1, 3, 2, 4, 5).reshape(frames, rows // 2, cols // 2, 4 * chans)


def attend(query_block, key_rows, value_rows):
    logits = jnp.einsum(
        "bhd,khd->hbk", query_block, key_rows, preferred_element_type=jnp.float32
    ) / math.sqrt(HS)
    expd = jnp.exp(logits - jnp.max(logits, -1, keepdims=True))
    weights = (expd / jnp.sum(expd, -1, keepdims=True)).astype(jnp.bfloat16)
    return jnp.einsum(
        "hbk,khd->bhd", weights, value_rows, preferred_element_type=jnp.float32
    ).astype(jnp.bfloat16)


def shards(
    video,
    conv_weight,
    latent_weight,
    embed_weight,
    modulation,
    qkv_weight,
    qk_gain,
    text,
    text_weight,
):
    upper_rim = shifted(video[:, -1:], "ctx", 1)
    framed = jnp.concatenate([upper_rim, video], 1)
    framed = jnp.concatenate([framed[:1], framed[:1], framed], 0)
    framed = jnp.pad(framed, ((0, 0), (0, 0), (1, 0), (0, 0)))
    conv = lax.conv_general_dilated(
        framed[None],
        conv_weight,
        (1, 2, 2),
        "VALID",
        dimension_numbers=("NDHWC", "DHWIO", "NDHWC"),
        preferred_element_type=jnp.float32,
    )[0]
    activated = jax.nn.silu(conv).astype(jnp.bfloat16)
    latent = jnp.dot(activated, latent_weight, preferred_element_type=jnp.float32).astype(
        jnp.bfloat16
    )
    tile_patches = patchify(latent)
    width_in = tile_patches.shape[3]
    token_rows = lax.all_to_all(
        tile_patches, "ctx", split_axis=0, concat_axis=1, tiled=True
    ).reshape(-1, width_in)
    embedded = jnp.dot(token_rows, embed_weight, preferred_element_type=jnp.float32)
    stream = (layer_norm(embedded) * (1.0 + modulation[1]) + modulation[0]).astype(jnp.bfloat16)
    text_stream = (
        layer_norm(text.astype(jnp.float32)) * (1.0 + modulation[3]) + modulation[2]
    ).astype(jnp.bfloat16)
    text_count = text.shape[0]
    local_heads = qkv_weight.shape[2] // HS
    flat_weight = qkv_weight.reshape(D, -1)
    projected = jnp.dot(
        lax.all_gather(stream, "ctx", axis=0, tiled=True),
        flat_weight,
        preferred_element_type=jnp.float32,
    )
    count = projected.shape[0]
    projected = projected.reshape(count, 3, local_heads, HS)
    queries = head_norm(projected[:, 0], qk_gain[0]).astype(jnp.bfloat16)
    keys_own = head_norm(projected[:, 1], qk_gain[1]).astype(jnp.bfloat16)
    values_own = projected[:, 2].astype(jnp.bfloat16)
    text_projected = jnp.dot(
        text_stream, text_weight.reshape(D, -1), preferred_element_type=jnp.float32
    )
    text_projected = text_projected.reshape(text_count, 2, local_heads, HS)
    text_keys = head_norm(text_projected[:, 0], qk_gain[1]).astype(jnp.bfloat16)
    text_values = text_projected[:, 1].astype(jnp.bfloat16)
    key_rows = jnp.concatenate([text_keys, keys_own], 0)
    value_rows = jnp.concatenate([text_values, values_own], 0)
    block = 512 if count % 512 == 0 else count
    blocks = queries.reshape(count // block, block, local_heads, HS)
    result = lax.map(lambda query_block: attend(query_block, key_rows, value_rows), blocks)
    result = result.reshape(count, local_heads * HS)
    return lax.all_to_all(result, "ctx", split_axis=0, concat_axis=1, tiled=True)


def solution(mesh):
    in_specs = (
        P("dp", "ctx", None, None),
        P(),
        P(),
        P(),
        P("dp", None),
        P(None, None, "ctx"),
        P(),
        P("dp", None),
        P(None, None, "ctx"),
    )
    out_specs = P(("dp", "ctx"), None)
    return jax.shard_map(shards, mesh=mesh, in_specs=in_specs, out_specs=out_specs, check_vma=False)
```

profile of v0, /device:TPU:0, one launch (start us, length us, event | category | flops | bytes accessed | tf_op | source)
XLA Modules:
  0.0 192.1 jit_solution(4728737379839621711)
XLA Ops:
  7.6 4.8 %collective-permute-start = (bf16[8,1,64,128]{3,2,1,0:T(8,128)(2,1)S(1)}, bf16[8,1,64,128]{3,2,1,0:T(8,128)(2,1)S(1)}, u32[]{:S(2)}, u32[]{:S(2)}) collective-permute-start(bf16[8,1,64,128]{3,2,1,0:T(8,128)(2,1)S(1)} %slice.43), channel_id=1, source_target_pairs={{0,1},{1,2},{2,3},{4,5},{5,6},{6,7},{8,9},{9,10},{10,11},{12,13},{... | collective-permute-start | bytes 393224 | tf_op jit(solution)/shard_map/ppermute | solution.py:14
  12.4 2.7 %collective-permute-done = bf16[8,1,64,128]{3,2,1,0:T(8,128)(2,1)S(1)} collective-permute-done((bf16[8,1,64,128]{3,2,1,0:T(8,128)(2,1)S(1)}, bf16[8,1,64,128]{3,2,1,0:T(8,128)(2,1)S(1)}, u32[]{:S(2)}, u32[]{:S(2)}) %collective-permute-start) | collective-permute-done | bytes 131104 | tf_op jit(solution)/shard_map/ppermute | solution.py:14
  18.7 4.6 %reshape.97 = bf16[10,9,1,8,10,128]{5,4,3,1,0,2:T(8,128)(2,1)} reshape(bf16[10,9,1,80,128]{4,3,1,0,2:T(8,128)(2,1)} %pad.5) | data formatting | bytes 3686400 | tf_op jit(solution)/shard_map/conv_general_dilated | solution.py:58
  23.3 2.4 %copy.26 = bf16[10,9,1,8,10,128]{5,3,4,1,0,2:T(8,128)(2,1)S(1)} copy(bf16[10,9,1,8,10,128]{5,4,3,1,0,2:T(8,128)(2,1)} %reshape.97) | data formatting | bytes 3686400 | tf_op jit(solution)/shard_map/conv_general_dilated | solution.py:58
  25.9 2.6 %fusion.57 = f32[8,4,8,5,256]{4,2,3,1,0:T(8,128)S(1)} fusion(bf16[3,3,3,128,256]{4,3,2,1,0:T(8,128)(2,1)S(1)} %copy-done, bf16[10,9,1,7,2,128]{5,3,4,1,0,2:T(8,128)(2,1)S(1)} %slice.59, bf16[10,9,1,8,10,128]{5,3,4,1,0,2:T(8,128)(2,1)S(1)} %copy.26, pred[8,5]{0,1:T(8,128)(4,1)S(1)} %copy-done.9), kind=kOutput, calls=%fused_computation.60 | convolution fusion | flops 2271887360 | bytes 5245992 | tf_op jit(solution)/shard_map/conv_general_dilated | solution.py:58
  31.5 4.7 %all-to-all-start = ((bf16[4,2,2048]{2,1,0:T(2,128)(2,1)}), bf16[4,2,2048]{2,1,0:T(2,128)(2,1)S(1)}, u32[]{:S(2)}, u32[]{:S(2)}) async-start(bf16[4,2,2048]{2,1,0:T(2,128)(2,1)} %reshape.112), calls=%async_computation | async-start | bytes 65536 | tf_op jit(solution)/shard_map/all_to_all | solution.py:72
  36.2 4.7 %all-to-all-done = bf16[4,2,2048]{2,1,0:T(2,128)(2,1)S(1)} async-done(((bf16[4,2,2048]{2,1,0:T(2,128)(2,1)}), bf16[4,2,2048]{2,1,0:T(2,128)(2,1)S(1)}, u32[]{:S(2)}, u32[]{:S(2)}) %all-to-all-start) | async-done | bytes 32800 | tf_op jit(solution)/shard_map/all_to_all | solution.py:72
  42.2 1.9 add_convert_fusion
  44.1 12.9 %copy.32 = bf16[3072,3,512]{0,2,1:T(8,128)(2,1)} copy(bf16[3072,3,512]{2,0,1:T(8,128)(2,1)} %param.16) | data formatting | bytes 18874368 | tf_op args[5]
  57.0 7.5 %copy.47 = bf16[384,8,2,512]{3,1,2,0:T(8,128)(2,1)} copy(bf16[384,8,2,512]{3,2,1,0:T(2,128)(2,1)} %bitcast.112) | data formatting | bytes 12582912
  64.5 8.8 %copy.35 = bf16[1024,3072]{1,0:T(8,128)(2,1)} copy(bf16[1024,3072]{0,1:T(8,128)(2,1)} %bitcast.109) | data formatting | bytes 12582912 | tf_op jit(solution)/shard_map/dot_general | solution.py:93
  74.2 4.0 %fusion.51 = f32[256,2,4,128]{3,0,2,1:T(8,128)S(1)} fusion(bf16[2,4,128,3072]{3,2,1,0:T(8,128)(2,1)} %bitcast.113, bf16[256,3072]{1,0:T(8,128)(2,1)S(1)} %copy-done.2, f32[3072]{0:T(1024)S(1)} %bitcast.124, f32[3072]{0:T(1024)S(1)} %bitcast.123, f32[256]{0:T(256)S(1)} %add_rsqrt_fusion.3, f32[256]{0:T(256)S(1)} %broadcast_multiply_fusion), kind=kOutput, calls=%fused_computation.55 | convolution fusion | flops 1615331328 | bytes 8939520 | tf_op jit(solution)/shard_map/dot_general | solution.py:93
  78.7 35.2 %all-gather.2.cloned.1.call-done = bf16[1024,3072]{1,0:T(8,128)(2,1)} async-done(((bf16[256,3072]{1,0:T(8,128)(2,1)}), bf16[1024,3072]{1,0:T(8,128)(2,1)}) %all-gather.2.cloned.1.call-update) | async-done | bytes 6291472 | tf_op jit(solution)/shard_map/all_gather | solution.py:84
  113.9 13.3 %fusion.26 = f32[1024,3,4,128]{3,0,2,1:T(8,128)S(1)} fusion(bf16[3,4,128,3072]{3,2,1,0:T(8,128)(2,1)} %bitcast.110, bf16[1024,3072]{1,0:T(8,128)(2,1)} %all-gather.2.cloned.1.call-done), kind=kOutput, calls=%fused_computation.19 | convolution fusion | flops 9663676416 | bytes 22020096 | tf_op jit(solution)/shard_map/dot_general | solution.py:83
  129.3 1.5 fusion.46
  132.1 31.1 %while.10 = (s32[]{:T(128)}, bf16[2,512,4,128]{3,2,1,0:T(4,128)(2,1)}, bf16[2,512,4,128]{3,1,2,0:T(8,128)(2,1)}, bf16[1280,4,128]{2,0,1:T(8,128)(2,1)S(1)}, bf16[1280,4,128]{2,0,1:T(8,128)(2,1)}, /*index=5*/s32[]{:T(128)}) while((s32[]{:T(128)}, bf16[2,512,4,128]{3,2,1,0:T(4,128)(2,1)}, bf16[2,512,4,128]{3,1,2,0:T(8,128)(2,1)}, ...), condition=%wide.region_10.11_spmd, body=%wide.region_7.10_spmd.sunk | while | flops 1355547904 | bytes 34095744 | solution.py:103
  132.1 8.1 %fusion.90 = (f32[4,512]{1,0:T(4,128)S(1)}, f32[4,512,1280]{2,1,0:T(8,128)}) fusion(bf16[1280,4,128]{2,0,1:T(8,128)(2,1)S(1)} %get-tuple-element.107, bf16[2,512,4,128]{3,1,2,0:T(8,128)(2,1)} %get-tuple-element.106, s32[]{:T(128)} %get-tuple-element.98), kind=kOutput, calls=%fused_computation.91.clone.1 | convolution fusion | flops 678954240 | bytes 12329472 | tf_op jit(solution)/shard_map/while/body/eval_jaxpr/sub | solution.py:36
  140.3 6.0 %fusion.91 = bf16[1,512,4,128]{3,1,2,0:T(8,128)(2,1)S(1)} fusion(bf16[1280,4,128]{2,0,1:T(8,128)(2,1)} %get-tuple-element.108, f32[4,512,1280]{2,1,0:T(8,128)} %get-tuple-element.90, f32[4,512]{1,0:T(4,128)S(1)} %get-tuple-element.91), kind=kOutput, calls=%fused_computation.8.clone.1 | convolution fusion | flops 676593664 | bytes 12328960 | tf_op jit(solution)/shard_map/while/body/eval_jaxpr/hbk,khd->bhd/dot_general | solution.py:38
  147.7 8.1 %fusion.90 = (f32[4,512]{1,0:T(4,128)S(1)}, f32[4,512,1280]{2,1,0:T(8,128)}) fusion(bf16[1280,4,128]{2,0,1:T(8,128)(2,1)S(1)} %get-tuple-element.107, bf16[2,512,4,128]{3,1,2,0:T(8,128)(2,1)} %get-tuple-element.106, s32[]{:T(128)} %get-tuple-element.98), kind=kOutput, calls=%fused_computation.91.clone.1 | convolution fusion | flops 678954240 | bytes 12329472 | tf_op jit(solution)/shard_map/while/body/eval_jaxpr/sub | solution.py:36
  155.8 6.0 %fusion.91 = bf16[1,512,4,128]{3,1,2,0:T(8,128)(2,1)S(1)} fusion(bf16[1280,4,128]{2,0,1:T(8,128)(2,1)} %get-tuple-element.108, f32[4,512,1280]{2,1,0:T(8,128)} %get-tuple-element.90, f32[4,512]{1,0:T(4,128)S(1)} %get-tuple-element.91), kind=kOutput, calls=%fused_computation.8.clone.1 | convolution fusion | flops 676593664 | bytes 12328960 | tf_op jit(solution)/shard_map/while/body/eval_jaxpr/hbk,khd->bhd/dot_general | solution.py:38
  163.2 1.5 all_to_all.28
  164.7 17.7 %all_to_all.34 = bf16[4,256,512]{2,1,0:T(8,128)(2,1)} all-to-all(bf16[4,256,512]{2,1,0:T(8,128)(2,1)S(1)} %all_to_all.28), channel_id=1, replica_groups=mesh['dp'=8,'ctx'=4] {'ctx'}, dimensions={0} | all-to-all | bytes 2097152 | tf_op jit(solution)/shard_map/all_to_all | solution.py:105
  182.4 1.5 copy.37
  183.9 1.4 copy.38
  (66 shorter events, 16.4 us)
Async XLA Ops:
  6.5 19.3 %copy-start = (bf16[3,3,3,128,256]{4,3,2,1,0:T(8,128)(2,1)S(1)}, bf16[3,3,3,128,256]{4,3,2,1,0:T(8,128)(2,1)}, u32[]{:S(2)}) copy-start(bf16[3,3,3,128,256]{4,3,2,1,0:T(8,128)(2,1)} %param.12) | copy-start | bytes 5308420
  7.6 7.6 %collective-permute-start = (bf16[8,1,64,128]{3,2,1,0:T(8,128)(2,1)S(1)}, bf16[8,1,64,128]{3,2,1,0:T(8,128)(2,1)S(1)}, u32[]{:S(2)}, u32[]{:S(2)}) collective-permute-start(bf16[8,1,64,128]{3,2,1,0:T(8,128)(2,1)S(1)} %slice.43), channel_id=1, source_target_pairs={{0,1},{1,2},{2,3},{4,5},{5,6},{6,7},{8,9},{9,10},{10,11},{12,13},{... | collective-permute-start | bytes 393224 | tf_op jit(solution)/shard_map/ppermute | solution.py:14
  23.3 2.6 %copy-start.9 = (pred[8,5]{0,1:T(8,128)(4,1)S(1)}, pred[8,5]{0,1:T(8,128)(4,1)}, u32[]{:S(2)}) copy-start(pred[8,5]{0,1:T(8,128)(4,1)} %constant.50) | copy-start | bytes 124
  28.5 1.1 copy-start.8
  28.5 7.7 %copy-start.6 = (f32[4,3072]{1,0:T(4,128)S(1)}, f32[4,3072]{1,0:T(4,128)}, u32[]{:S(2)}) copy-start(f32[4,3072]{1,0:T(4,128)} %param.15) | copy-start | bytes 147460
  29.3 11.8 %copy-start.5 = (bf16[64,3072]{1,0:T(8,128)(2,1)S(1)}, bf16[64,3072]{1,0:T(8,128)(2,1)}, u32[]{:S(2)}) copy-start(bf16[64,3072]{1,0:T(8,128)(2,1)} %param.14) | copy-start | bytes 1179652
  31.5 9.5 %all-to-all-start = ((bf16[4,2,2048]{2,1,0:T(2,128)(2,1)}), bf16[4,2,2048]{2,1,0:T(2,128)(2,1)S(1)}, u32[]{:S(2)}, u32[]{:S(2)}) async-start(bf16[4,2,2048]{2,1,0:T(2,128)(2,1)} %reshape.112), calls=%async_computation | async-start | bytes 65536 | tf_op jit(solution)/shard_map/all_to_all | solution.py:72
  36.2 77.7 %all-gather.2.cloned.1.call-start = ((), (), s32[]{:S(2)}) async-start(), calls=%async_computation.2 | async-start | bytes 7864320 | tf_op jit(solution)/shard_map/all_gather | solution.py:84
  64.5 8.8 %copy-start.2 = (bf16[256,3072]{1,0:T(8,128)(2,1)S(1)}, bf16[256,3072]{1,0:T(8,128)(2,1)}, u32[]{:S(2)}) copy-start(bf16[256,3072]{1,0:T(8,128)(2,1)} %param.18) | copy-start | bytes 4718596
  74.2 4.2 %copy-start.7 = (f32[2,128]{1,0:T(2,128)S(1)}, f32[2,128]{1,0:T(2,128)}, u32[]{:S(2)}) copy-start(f32[2,128]{1,0:T(2,128)} %param.17) | copy-start | bytes 3076
  140.3 6.0 %copy-start.3 = (bf16[2,512,4,128]{3,2,1,0:T(4,128)(2,1)S(1)}, bf16[2,512,4,128]{3,2,1,0:T(4,128)(2,1)}, u32[]{:S(2)}) copy-start(bf16[2,512,4,128]{3,2,1,0:T(4,128)(2,1)} %get-tuple-element.99) | copy-start | bytes 3145732 | tf_op jit(solution)/shard_map/while
  146.7 1.0 copy-start.4
  155.8 6.0 %copy-start.3 = (bf16[2,512,4,128]{3,2,1,0:T(4,128)(2,1)S(1)}, bf16[2,512,4,128]{3,2,1,0:T(4,128)(2,1)}, u32[]{:S(2)}) copy-start(bf16[2,512,4,128]{3,2,1,0:T(4,128)(2,1)} %get-tuple-element.99) | copy-start | bytes 3145732 | tf_op jit(solution)/shard_map/while
  162.2 1.0 copy-start.4
  164.7 20.6 %copy-start.1 = (bf16[3,3,3,128,256]{4,3,2,1,0:T(8,128)(2,1)S(1)}, bf16[3,3,3,128,256]{4,3,2,1,0:T(8,128)(2,1)}, u32[]{:S(2)}) copy-start(bf16[3,3,3,128,256]{4,3,2,1,0:T(8,128)(2,1)} %param.12) | copy-start | bytes 5308420
Sparse Core Ops, SparseCore 0:
  44.2 69.6 all-gather.1
where the time goes:
time: 193 us; the launch traced here: 192 us
  local copies, waits for them, and re-layouts  49.8 us (26%)
  matrix products  49.2 us (25%)
  waiting for transfers between devices  42.6 us (22%)
  blocking collectives  17.7 us (9%)
  between operations  13.7 us (7%)
  starting transfers between devices  9.56 us (5%)
  other arithmetic  9.49 us (5%)
    all_gather x1, waiting for transfers between devices, shards(): lax.all_gather(stream, 'ctx', axis=0, tiled=True)  35.2 us
    unnamed x21, local copies, waits for them, and re-layouts  21.3 us
    all_to_all x1, blocking collectives, shards(): lax.all_to_all(result, 'ctx', split_axis=0, concat_axis=1, tiled=True)  17.7 us
    sub x2, matrix products, attend(): expd = jnp.exp(logits - jnp.max(logits, -1, keepdims=True))  16.3 us
    dot_general x1, matrix products, shards(): jnp.dot(lax.all_gather(stream, 'ctx', axis=0, tiled=True), flat_weight, p...  13.3 us
    dot_general x2, matrix products, attend(): jnp.einsum('hbk,khd->bhd', weights, value_rows, preferred_element_type=jn...  11.9 us
    dot_general x1, local copies, waits for them, and re-layouts, shards(): jnp.dot(text_stream, text_weight.reshape(D, -1), preferred_element_type=j...  8.79 us
    conv_general_dilated x4, local copies, waits for them, and re-layouts, shards(): lax.conv_general_dilated(framed[None], conv_weight, (1, 2, 2), 'VALID', d...  7.91 us
  transfers between devices with their start and end apart: 3, of which 3 were waited for; matrix products, arithmetic and copies ran while one was open for 18% of the time, Pallas kernels for 0%

commit v1 on v0

--- a/solution.py
+++ b/solution.py
@@ -6,6 +6,28 @@
 
 D = 3072
 HS = 128
+
+
+def in_order(tiles, dim):
+    shape = list(tiles.shape[1:])
+    shape[dim] *= tiles.shape[0]
+    return jnp.moveaxis(tiles, 0, dim).reshape(shape)
+
+
+def collected_by_bits(x, axis):
+    count = lax.axis_size(axis)
+    pieces = x[None]
+    for level in range(count.bit_length() - 1):
+        bit = 1 << level
+        received = lax.ppermute(pieces, axis, [(i, i ^ bit) for i in range(count)])
+        both = jnp.stack([pieces, received])
+        upper = lax.axis_index(axis) >> level & 1
+        pieces = jnp.where(upper == 0, both, both[::-1]).reshape(-1, *x.shape)
+    return pieces
+
+
+def gather_by_bits(x, axis, dim):
+    return in_order(collected_by_bits(x, axis), dim)
 
 
 def shifted(x, axis, by):
@@ -81,9 +103,7 @@
     local_heads = qkv_weight.shape[2] // HS
     flat_weight = qkv_weight.reshape(D, -1)
     projected = jnp.dot(
-        lax.all_gather(stream, "ctx", axis=0, tiled=True),
-        flat_weight,
-        preferred_element_type=jnp.float32,
+        gather_by_bits(stream, "ctx", 0), flat_weight, preferred_element_type=jnp.float32
     )
     count = projected.shape[0]
     projected = projected.reshape(count, 3, local_heads, HS)

time: 193 us -> 215 us (1.11)
  waiting for transfers between devices: 42.6 us -> 67.9 us
  other arithmetic: 9.49 us -> 24.6 us
  between operations: 13.7 us -> 0.38 us
  blocking collectives: 17.7 us -> 13.6 us
    ppermute x0 -> x2, waiting for transfers between devices: none -> 61.1 us  [collected_by_bits(): received = lax.ppermute(pieces, axis, [(i, i ^ bit) for i in range(count)])]
    all_gather x1 -> x0, waiting for transfers between devices: 35.2 us -> none  [shards(): lax.all_gather(stream, 'ctx', axis=0, tiled=True)]
    another operation x0 -> x4, other arithmetic: none -> 7.69 us  [collected_by_bits(): both = jnp.stack([pieces, received])]
    select_n x0 -> x1, other arithmetic: none -> 4.36 us  [collected_by_bits(): pieces = jnp.where(upper == 0, both, both[::-1]).reshape(-1, *x.shape)]
    all_to_all x1, blocking collectives: 17.7 us -> 13.6 us  [shards(): lax.all_to_all(result, 'ctx', split_axis=0, concat_axis=1, tiled=True)]
    unnamed x21 -> x37, local copies, waits for them, and re-layouts: 21.3 us -> 21.1 us
  transfers between devices with their start and end apart: 3 -> 4, of which waited for: 3 -> 4; matrix products, arithmetic and copies ran while one was open for 18% -> 18% of each run, Pallas kernels for 0% -> 0%
where the time goes in v1:
time: 215 us; the launch traced here: 214 us
  waiting for transfers between devices  67.9 us (32%)
  local copies, waits for them, and re-layouts  49.2 us (23%)
  matrix products  47.4 us (22%)
  other arithmetic  24.6 us (11%)
  blocking collectives  13.6 us (6%)
  starting transfers between devices  11 us (5%)
    ppermute x2, waiting for transfers between devices, collected_by_bits(): received = lax.ppermute(pieces, axis, [(i, i ^ bit) for i in range(count)])  61.1 us
    unnamed x37, local copies, waits for them, and re-layouts  21.1 us
    sub x2, matrix products, attend(): expd = jnp.exp(logits - jnp.max(logits, -1, keepdims=True))  16.3 us
    all_to_all x1, blocking collectives, shards(): lax.all_to_all(result, 'ctx', split_axis=0, concat_axis=1, tiled=True)  13.6 us
    dot_general x1, matrix products, shards(): jnp.dot(gather_by_bits(stream, 'ctx', 0), flat_weight, preferred_element_...  12.3 us
    dot_general x2, matrix products, attend(): jnp.einsum('hbk,khd->bhd', weights, value_rows, preferred_element_type=jn...  11.1 us
    dot_general x1, local copies, waits for them, and re-layouts, shards(): jnp.dot(text_stream, text_weight.reshape(D, -1), preferred_element_type=j...  8.7 us
    conv_general_dilated x4, local copies, waits for them, and re-layouts, shards(): lax.conv_general_dilated(framed[None], conv_weight, (1, 2, 2), 'VALID', d...  7.92 us
  transfers between devices with their start and end apart: 4, of which 4 were waited for; matrix products, arithmetic and copies ran while one was open for 18% of the time, Pallas kernels for 0%

profile of v1, /device:TPU:0, one launch (start us, length us, event | category | flops | bytes accessed | tf_op | source)
XLA Modules:
  0.0 214.1 jit_solution(9160654831365593848)
XLA Ops:
  1.1 4.8 %collective-permute-start = (bf16[8,1,64,128]{3,2,1,0:T(8,128)(2,1)S(1)}, bf16[8,1,64,128]{3,2,1,0:T(8,128)(2,1)S(1)}, u32[]{:S(2)}, u32[]{:S(2)}) collective-permute-start(bf16[8,1,64,128]{3,2,1,0:T(8,128)(2,1)S(1)} %slice.43), channel_id=1, source_target_pairs={{0,1},{1,2},{2,3},{4,5},{5,6},{6,7},{8,9},{9,10},{10,11},{12,13},{... | collective-permute-start | bytes 393224 | tf_op jit(solution)/shard_map/ppermute | solution.py:36
  5.9 2.7 %collective-permute-done = bf16[8,1,64,128]{3,2,1,0:T(8,128)(2,1)S(1)} collective-permute-done((bf16[8,1,64,128]{3,2,1,0:T(8,128)(2,1)S(1)}, bf16[8,1,64,128]{3,2,1,0:T(8,128)(2,1)S(1)}, u32[]{:S(2)}, u32[]{:S(2)}) %collective-permute-start) | collective-permute-done | bytes 131104 | tf_op jit(solution)/shard_map/ppermute | solution.py:36
  12.2 4.6 %reshape.101 = bf16[10,9,1,8,10,128]{5,4,3,1,0,2:T(8,128)(2,1)} reshape(bf16[10,9,1,80,128]{4,3,1,0,2:T(8,128)(2,1)} %pad.5) | data formatting | bytes 3686400 | tf_op jit(solution)/shard_map/conv_general_dilated | solution.py:80
  16.8 2.4 %copy.26 = bf16[10,9,1,8,10,128]{5,3,4,1,0,2:T(8,128)(2,1)S(1)} copy(bf16[10,9,1,8,10,128]{5,4,3,1,0,2:T(8,128)(2,1)} %reshape.101) | data formatting | bytes 3686400 | tf_op jit(solution)/shard_map/conv_general_dilated | solution.py:80
  19.4 2.6 %fusion.57 = f32[8,4,8,5,256]{4,2,3,1,0:T(8,128)S(1)} fusion(bf16[3,3,3,128,256]{4,3,2,1,0:T(8,128)(2,1)S(1)} %copy-done, bf16[10,9,1,7,2,128]{5,3,4,1,0,2:T(8,128)(2,1)S(1)} %slice.59, bf16[10,9,1,8,10,128]{5,3,4,1,0,2:T(8,128)(2,1)S(1)} %copy.26, pred[8,5]{0,1:T(8,128)(4,1)S(1)} %copy-done.12), kind=kOutput, calls=%fused_computation.64 | convolution fusion | flops 2271887360 | bytes 5245992 | tf_op jit(solution)/shard_map/conv_general_dilated | solution.py:80
  24.9 4.7 %all-to-all-start = ((bf16[4,2,2048]{2,1,0:T(2,128)(2,1)}), bf16[4,2,2048]{2,1,0:T(2,128)(2,1)S(1)}, u32[]{:S(2)}, u32[]{:S(2)}) async-start(bf16[4,2,2048]{2,1,0:T(2,128)(2,1)} %reshape.116), calls=%async_computation | async-start | bytes 65536 | tf_op jit(solution)/shard_map/all_to_all | solution.py:94
  30.3 4.1 %all-to-all-done = bf16[4,2,2048]{2,1,0:T(2,128)(2,1)S(1)} async-done(((bf16[4,2,2048]{2,1,0:T(2,128)(2,1)}), bf16[4,2,2048]{2,1,0:T(2,128)(2,1)S(1)}, u32[]{:S(2)}, u32[]{:S(2)}) %all-to-all-start) | async-done | bytes 32800 | tf_op jit(solution)/shard_map/all_to_all | solution.py:94
  38.9 32.7 %collective-permute-done.1 = bf16[1,256,3072]{2,1,0:T(8,128)(2,1)} collective-permute-done((bf16[1,256,3072]{2,1,0:T(8,128)(2,1)}, bf16[1,256,3072]{2,1,0:T(8,128)(2,1)}, u32[]{:S(2)}, u32[]{:S(2)}) %collective-permute-start.1) | collective-permute-done | bytes 1572896 | tf_op jit(solution)/shard_map/ppermute | solution.py:22
  73.4 2.7 %fusion.37 = (bf16[1,2,256,3072]{3,2,1,0:T(8,128)(2,1)S(1)}, bf16[2,256,3072]{2,1,0:T(8,128)(2,1)}) fusion(bf16[2,1,256,3072]{3,2,1,0:T(8,128)(2,1)S(1)} %pad_maximum_fusion.1, pred[]{:T(512)S(6)} %eq.7), kind=kLoop, calls=%fused_computation.40 | loop fusion | flops 1572864 | bytes 9437185 | tf_op jit(solution)/shard_map/stack;reshape | solution.py:23
  76.7 12.7 %copy.32 = bf16[3072,3,512]{0,2,1:T(8,128)(2,1)} copy(bf16[3072,3,512]{2,0,1:T(8,128)(2,1)} %param.16) | data formatting | bytes 18874368 | tf_op args[5]
  89.4 7.4 %copy.47 = bf16[384,8,2,512]{3,1,2,0:T(8,128)(2,1)} copy(bf16[384,8,2,512]{3,2,1,0:T(2,128)(2,1)} %bitcast.125) | data formatting | bytes 12582912
  96.9 8.7 %copy.35 = bf16[1024,3072]{1,0:T(8,128)(2,1)} copy(bf16[1024,3072]{0,1:T(8,128)(2,1)} %bitcast.120) | data formatting | bytes 12582912 | tf_op jit(solution)/shard_map/dot_general | solution.py:113
  107.4 2.0 fusion.32
  109.4 4.0 %fusion.51 = f32[256,2,4,128]{3,0,2,1:T(8,128)S(1)} fusion(bf16[2,4,128,3072]{3,2,1,0:T(8,128)(2,1)} %bitcast.126, bf16[256,3072]{1,0:T(8,128)(2,1)S(1)} %copy-done.2, f32[3072]{0:T(1024)S(1)} %bitcast.140, f32[3072]{0:T(1024)S(1)} %bitcast.139, f32[256]{0:T(256)S(1)} %add_rsqrt_fusion.3, f32[256]{0:T(256)S(1)} %broadcast_multiply_fusion), kind=kOutput, calls=%fused_computation.59 | convolution fusion | flops 1615331328 | bytes 8939520 | tf_op jit(solution)/shard_map/dot_general | solution.py:113
  114.7 28.4 %collective-permute-done.2 = bf16[2,256,3072]{2,1,0:T(8,128)(2,1)} collective-permute-done((bf16[2,256,3072]{2,1,0:T(8,128)(2,1)}, bf16[2,256,3072]{2,1,0:T(8,128)(2,1)}, u32[]{:S(2)}, u32[]{:S(2)}) %collective-permute-start.2) | collective-permute-done | bytes 3145760 | tf_op jit(solution)/shard_map/ppermute | solution.py:22
  143.0 2.6 %pad_maximum_fusion = bf16[2,2,256,3072]{3,2,1,0:T(8,128)(2,1)S(1)} fusion(bf16[1,2,256,3072]{3,2,1,0:T(8,128)(2,1)} %bitcast.21, bf16[1,2,256,3072]{3,2,1,0:T(8,128)(2,1)S(1)} %get-tuple-element.47), kind=kLoop, calls=%fused_computation.20 | loop fusion | flops 3145728 | bytes 12582912 | tf_op jit(solution)/shard_map/stack | solution.py:23
  145.6 4.4 %reverse_select_fusion = bf16[2,2,256,3072]{3,2,1,0:T(8,128)(2,1)} fusion(bf16[2,2,256,3072]{3,2,1,0:T(8,128)(2,1)S(1)} %pad_maximum_fusion, pred[]{:T(512)S(6)} %eq.6), kind=kLoop, calls=%fused_computation.19 | loop fusion | flops 3145728 | bytes 12582913 | tf_op jit(solution)/shard_map/jit(_where)/select_n | solution.py:25
  150.0 12.3 %fusion.74 = f32[1024,3,4,128]{3,0,2,1:T(8,128)S(1)} fusion(bf16[1024,3072,1,1]{1,0,3,2:T(8,128)(2,1)} %bitcast.127, bf16[3,4,128,3072]{3,2,1,0:T(8,128)(2,1)S(1)} %bitcast.123), kind=kOutput, calls=%fused_computation.97 | convolution fusion | flops 9663676416 | bytes 22020096 | tf_op jit(solution)/shard_map/dot_general | solution.py:105
  166.2 29.8 %while.10 = (s32[]{:T(128)}, bf16[2,512,4,128]{3,2,1,0:T(4,128)(2,1)}, bf16[2,512,4,128]{3,1,2,0:T(8,128)(2,1)}, bf16[1280,4,128]{2,0,1:T(8,128)(2,1)S(1)}, bf16[1280,4,128]{2,0,1:T(8,128)(2,1)S(1)}, /*index=5*/s32[]{:T(128)}) while((s32[]{:T(128)}, bf16[2,512,4,128]{3,2,1,0:T(4,128)(2,1)}, bf16[2,512,4,128]{3,1,2,0:T(8,128)(2,1)}, ...), condition=%wide.region_10.11_spmd, body=%wide.region_7.10_spmd.sunk | while | flops 1355547904 | bytes 25707588 | solution.py:123
  166.2 8.1 %fusion.94 = (f32[4,512]{1,0:T(4,128)S(1)}, f32[4,512,1280]{2,1,0:T(8,128)}) fusion(bf16[1280,4,128]{2,0,1:T(8,128)(2,1)S(1)} %get-tuple-element.109, bf16[2,512,4,128]{3,1,2,0:T(8,128)(2,1)} %get-tuple-element.108, s32[]{:T(128)} %get-tuple-element.100), kind=kOutput, calls=%fused_computation.95.clone.1 | convolution fusion | flops 678954240 | bytes 12329472 | tf_op jit(solution)/shard_map/while/body/eval_jaxpr/sub | solution.py:58
  174.4 5.5 %fusion.95 = bf16[1,512,4,128]{3,1,2,0:T(8,128)(2,1)S(1)} fusion(bf16[1280,4,128]{2,0,1:T(8,128)(2,1)S(1)} %get-tuple-element.110, f32[4,512,1280]{2,1,0:T(8,128)} %get-tuple-element.92, f32[4,512]{1,0:T(4,128)S(1)} %get-tuple-element.93), kind=kOutput, calls=%fused_computation.8.clone.1 | convolution fusion | flops 676593664 | bytes 12328960 | tf_op jit(solution)/shard_map/while/body/eval_jaxpr/hbk,khd->bhd/dot_general | solution.py:60
  181.1 8.1 %fusion.94 = (f32[4,512]{1,0:T(4,128)S(1)}, f32[4,512,1280]{2,1,0:T(8,128)}) fusion(bf16[1280,4,128]{2,0,1:T(8,128)(2,1)S(1)} %get-tuple-element.109, bf16[2,512,4,128]{3,1,2,0:T(8,128)(2,1)} %get-tuple-element.108, s32[]{:T(128)} %get-tuple-element.100), kind=kOutput, calls=%fused_computation.95.clone.1 | convolution fusion | flops 678954240 | bytes 12329472 | tf_op jit(solution)/shard_map/while/body/eval_jaxpr/sub | solution.py:58
  189.3 5.5 %fusion.95 = bf16[1,512,4,128]{3,1,2,0:T(8,128)(2,1)S(1)} fusion(bf16[1280,4,128]{2,0,1:T(8,128)(2,1)S(1)} %get-tuple-element.110, f32[4,512,1280]{2,1,0:T(8,128)} %get-tuple-element.92, f32[4,512]{1,0:T(4,128)S(1)} %get-tuple-element.93), kind=kOutput, calls=%fused_computation.8.clone.1 | convolution fusion | flops 676593664 | bytes 12328960 | tf_op jit(solution)/shard_map/while/body/eval_jaxpr/hbk,khd->bhd/dot_general | solution.py:60
  197.6 13.6 %all_to_all.34 = bf16[4,256,512]{2,1,0:T(8,128)(2,1)} all-to-all(bf16[4,256,512]{2,1,0:T(8,128)(2,1)S(1)} %all_to_all.28), channel_id=1, replica_groups=mesh['dp'=8,'ctx'=4] {'ctx'}, dimensions={0} | all-to-all | bytes 2097152 | tf_op jit(solution)/shard_map/all_to_all | solution.py:125
  (81 shorter events, 28.7 us)
Async XLA Ops:
  0.0 19.3 %copy-start = (bf16[3,3,3,128,256]{4,3,2,1,0:T(8,128)(2,1)S(1)}, bf16[3,3,3,128,256]{4,3,2,1,0:T(8,128)(2,1)}, u32[]{:S(2)}) copy-start(bf16[3,3,3,128,256]{4,3,2,1,0:T(8,128)(2,1)} %param.12) | copy-start | bytes 5308420
  1.1 7.6 %collective-permute-start = (bf16[8,1,64,128]{3,2,1,0:T(8,128)(2,1)S(1)}, bf16[8,1,64,128]{3,2,1,0:T(8,128)(2,1)S(1)}, u32[]{:S(2)}, u32[]{:S(2)}) collective-permute-start(bf16[8,1,64,128]{3,2,1,0:T(8,128)(2,1)S(1)} %slice.43), channel_id=1, source_target_pairs={{0,1},{1,2},{2,3},{4,5},{5,6},{6,7},{8,9},{9,10},{10,11},{12,13},{... | collective-permute-start | bytes 393224 | tf_op jit(solution)/shard_map/ppermute | solution.py:36
  16.8 2.6 %copy-start.12 = (pred[8,5]{0,1:T(8,128)(4,1)S(1)}, pred[8,5]{0,1:T(8,128)(4,1)}, u32[]{:S(2)}) copy-start(pred[8,5]{0,1:T(8,128)(4,1)} %constant.56) | copy-start | bytes 124
  22.0 1.1 copy-start.11
  22.0 7.7 %copy-start.7 = (f32[4,3072]{1,0:T(4,128)S(1)}, f32[4,3072]{1,0:T(4,128)}, u32[]{:S(2)}) copy-start(f32[4,3072]{1,0:T(4,128)} %param.15) | copy-start | bytes 147460
  22.0 12.5 %copy-start.4 = (bf16[64,3072]{1,0:T(8,128)(2,1)S(1)}, bf16[64,3072]{1,0:T(8,128)(2,1)}, u32[]{:S(2)}) copy-start(bf16[64,3072]{1,0:T(8,128)(2,1)} %param.14) | copy-start | bytes 1179652
  24.9 9.5 %all-to-all-start = ((bf16[4,2,2048]{2,1,0:T(2,128)(2,1)}), bf16[4,2,2048]{2,1,0:T(2,128)(2,1)S(1)}, u32[]{:S(2)}, u32[]{:S(2)}) async-start(bf16[4,2,2048]{2,1,0:T(2,128)(2,1)} %reshape.116), calls=%async_computation | async-start | bytes 65536 | tf_op jit(solution)/shard_map/all_to_all | solution.py:94
  34.6 1.1 copy-start.5
  35.7 2.6 %copy-start.6 = (f32[1,3072]{1,0:T(1,128)S(1)}, f32[1,3072]{1,0:T(1,128)}, u32[]{:S(2)}) copy-start(f32[1,3072]{1,0:T(1,128)} %get-tuple-element.51) | copy-start | bytes 36868
  37.5 34.1 %collective-permute-start.1 = (bf16[1,256,3072]{2,1,0:T(8,128)(2,1)}, bf16[1,256,3072]{2,1,0:T(8,128)(2,1)}, u32[]{:S(2)}, u32[]{:S(2)}) collective-permute-start(bf16[1,256,3072]{2,1,0:T(8,128)(2,1)} %fusion.85), channel_id=1, source_target_pairs={{0,1},{1,0},{2,3},{3,2},{4,5},{5,4},{6,7},{7,6},{8,9},{9,8},{10,11... | collective-permute-start | bytes 4718600 | tf_op jit(solution)/shard_map/ppermute | solution.py:22
  76.1 66.9 %collective-permute-start.2 = (bf16[2,256,3072]{2,1,0:T(8,128)(2,1)}, bf16[2,256,3072]{2,1,0:T(8,128)(2,1)}, u32[]{:S(2)}, u32[]{:S(2)}) collective-permute-start(bf16[2,256,3072]{2,1,0:T(8,128)(2,1)} %get-tuple-element.48), channel_id=1, source_target_pairs={{0,2},{1,3},{2,0},{3,1},{4,6},{5,7},{6,4},{7,5},{8,10},{9,11},{10,... | collective-permute-start | bytes 9437192 | tf_op jit(solution)/shard_map/ppermute | solution.py:22
  105.6 3.8 %copy-start.2 = (bf16[256,3072]{1,0:T(8,128)(2,1)S(1)}, bf16[256,3072]{1,0:T(8,128)(2,1)}, u32[]{:S(2)}) copy-start(bf16[256,3072]{1,0:T(8,128)(2,1)} %param.18) | copy-start | bytes 4718596
  105.6 3.8 %copy-start.8 = (f32[1,3072]{1,0:T(1,128)S(1)}, f32[1,3072]{1,0:T(1,128)}, u32[]{:S(2)}) copy-start(f32[1,3072]{1,0:T(1,128)} %get-tuple-element.49) | copy-start | bytes 36868
  105.6 3.8 %copy-start.9 = (f32[1,3072]{1,0:T(1,128)S(1)}, f32[1,3072]{1,0:T(1,128)}, u32[]{:S(2)}) copy-start(f32[1,3072]{1,0:T(1,128)} %get-tuple-element.52) | copy-start | bytes 36868
  109.4 4.3 %copy-start.10 = (f32[2,128]{1,0:T(2,128)S(1)}, f32[2,128]{1,0:T(2,128)}, u32[]{:S(2)}) copy-start(f32[2,128]{1,0:T(2,128)} %param.17) | copy-start | bytes 3076
  143.0 7.0 %slice-start = ((s8[9437184]{0:T(1024)(128)(4,1)}), s8[4194304]{0:T(1024)(128)(4,1)S(1)}, s32[]{:S(2)}) async-start(s8[9437184]{0:T(1024)(128)(4,1)} %bitcast.121), calls=%async_computation.2 | async-start | bytes 8388608
  143.0 7.0 %slice-start.1 = ((s8[9437184]{0:T(1024)(128)(4,1)}), s8[4194304]{0:T(1024)(128)(4,1)S(1)}, s32[]{:S(2)}) async-start(s8[9437184]{0:T(1024)(128)(4,1)} %bitcast.121), calls=%async_computation.3 | async-start | bytes 8388608
  145.6 4.4 %slice-start.2 = ((s8[9437184]{0:T(1024)(128)(4,1)}), s8[1048576]{0:T(1024)(128)(4,1)S(1)}, s32[]{:S(2)}) async-start(s8[9437184]{0:T(1024)(128)(4,1)} %bitcast.121), calls=%async_computation.4 | async-start | bytes 2097152
  163.8 2.3 %copy-start.3 = (bf16[256,4,128]{2,0,1:T(8,128)(2,1)S(1)}, bf16[256,4,128]{2,0,1:T(8,128)(2,1)}, u32[]{:S(2)}) copy-start(bf16[256,4,128]{2,0,1:T(8,128)(2,1)} %multiply_convert_fusion.2) | copy-start | bytes 786436
  196.0 18.1 %copy-start.1 = (bf16[3,3,3,128,256]{4,3,2,1,0:T(8,128)(2,1)S(1)}, bf16[3,3,3,128,256]{4,3,2,1,0:T(8,128)(2,1)}, u32[]{:S(2)}) copy-start(bf16[3,3,3,128,256]{4,3,2,1,0:T(8,128)(2,1)} %param.12) | copy-start | bytes 5308420
